TPU v7x, 32 devices: a whole 2x2x4 slice. The times are simulated.
32 devices in a mesh: sect: 4 (over x, core), batch: 8 (over z, y).
Axes of the slice: x: 2, y: 2, z: 4, core: 2. Of those that a mesh axis runs over, the one named last changes fastest.
Arguments:
- warm: bfloat16 [8192, 640], P(('sect', 'batch')), may hold values from -6 to 6
- latents: float32 [4, 1024], P(None, 'batch'), may hold values from -6 to 6
- timesteps: int32 [5], replicated, may hold values from 300 to 599
- assign: int32 [8], P('batch'), may hold values from 0 to 7, each once
- prompts: bfloat16 [8, 640], P('batch'), may hold values from -6 to 6
- w_in: bfloat16 [2560, 2560], P('sect'), may hold values from -0.25 to 0.25
- time_w: bfloat16 [2560, 640], P('sect'), may hold values from -0.25 to 0.25
- w_out: bfloat16 [5120, 640], P(('sect', 'batch')), may hold values from -0.15625 to 0.15625
- conv_in_w: bfloat16 [4, 640], replicated, may hold values from -3 to 3
- conv_out_w: bfloat16 [4, 640], replicated, may hold values from -0.25 to 0.25
Outputs:
- segments: bfloat16 [8192, 640], P(('sect', 'batch'))
- final_latents: float32 [4, 1024], P('sect', 'batch')
Inputs may be any that keep to these rules, and one draw needn't show every extreme that they name: `assign`: each prompt is assigned to exactly one prompt batch.
All inputs are finite; a program needn't handle non-finite values.
Results may differ from a plain program's by a relative error of at most 0.015.
Values may be sent and summed in bfloat16 or wider, within the bound.
A program may use at most 64 MiB of HBM per device.

v0:
```python
import math
import jax
import jax.numpy as jnp
from jax import lax
from jax.sharding import PartitionSpec as P

guidance_scale = 3.0


def passed_along(shard, axis, by):
    devices = lax.axis_size(axis)
    pairs = [(i, i + by) for i in range(devices) if 0 <= i + by < devices]
    return lax.ppermute(shard, axis, pairs)


def from_behind(block, axis, distance):
    devices = range(lax.axis_size(axis))
    route = [((i - distance) % len(devices), i) for i in devices]
    return lax.ppermute(block, axis, route)


def broadcast(block, axis, source):
    block = jnp.where(lax.axis_index(axis) == source, block, jnp.zeros_like(block))
    return lax.psum(block, axis)


def sinusoid(time_value, channels):
    half_width = channels // 2
    frequency = jnp.exp(-math.log(10000.0) * jnp.arange(half_width, dtype=jnp.float32) / half_width)
    angles = time_value.astype(jnp.float32) * frequency
    return jnp.concatenate([jnp.cos(angles), jnp.sin(angles)])


def alpha_bar(time_value):
    phase_angle = (time_value.astype(jnp.float32) / 1000.0 + 0.008) / 1.008 * (math.pi / 2)
    return jnp.cos(phase_angle) ** 2


def rms_norm(values):
    return values * lax.rsqrt(jnp.mean(values * values, axis=-1, keepdims=True) + 1e-06)


def feed_block(inputs, time_vec, cond_rows, weight_in, weight_out, hidden_units):
    summed = inputs + time_vec + cond_rows
    normed = rms_norm(summed).astype(jnp.bfloat16)
    projected = jnp.dot(normed, weight_in, preferred_element_type=jnp.float32)
    hidden = (
        projected[:, :hidden_units] * jax.nn.gelu(projected[:, hidden_units:], approximate=False)
    ).astype(jnp.bfloat16)
    return (summed + jnp.dot(hidden, weight_out, preferred_element_type=jnp.float32)).astype(
        jnp.bfloat16
    )


def on_device(
    warm, latents, timesteps, assign, prompts, w_in, time_w, w_out, conv_in_w, conv_out_w
):
    section = lax.axis_index("sect")
    sect_count = lax.axis_size("sect")
    last_index = sect_count - 1
    w_out_all, table = (
        lax.all_gather(w_out, "batch", axis=0, tiled=True),
        lax.all_gather(prompts, "batch", axis=0, tiled=True),
    )
    positions = latents.shape[1]
    channels = warm.shape[1]
    hidden_units = w_out_all.shape[0]
    picker = (jnp.arange(table.shape[0], dtype=jnp.int32)[None, :] == assign[:, None]).astype(
        jnp.bfloat16
    )
    chosen = jnp.dot(picker, table, preferred_element_type=jnp.float32)
    cond = jnp.concatenate(
        [
            jnp.broadcast_to(chosen, (positions, channels)),
            jnp.zeros((positions, channels), jnp.float32),
        ],
        axis=0,
    )
    segment = warm
    latent = latents
    for step_index in range(timesteps.shape[0] - 1):
        time_now = timesteps[step_index]
        time_next = timesteps[step_index + 1]
        received = passed_along(segment, "sect", 1)
        skipped = from_behind(segment, "sect", -1)
        embedded = jax.nn.silu(sinusoid(time_now, channels)).astype(jnp.bfloat16)
        first = lax.dot_general(
            latent.astype(jnp.bfloat16),
            conv_in_w,
            (((0,), (0,)), ((), ())),
            preferred_element_type=jnp.float32,
        ).astype(jnp.bfloat16)
        first = jnp.concatenate([first, first], axis=0)
        inputs = jnp.where(section == 0, first, received).astype(jnp.float32)
        inputs = (inputs + skipped.astype(jnp.float32)) * 0.5
        time_vec = jnp.dot(embedded[None, :], time_w, preferred_element_type=jnp.float32)
        segment = feed_block(inputs, time_vec, cond, w_in, w_out_all, hidden_units)
        activated = jax.nn.silu(rms_norm(segment.astype(jnp.float32))).astype(jnp.bfloat16)
        noise = lax.dot_general(
            conv_out_w, activated, (((1,), (1,)), ((), ())), preferred_element_type=jnp.float32
        )
        guided = noise[:, positions:] + guidance_scale * (
            noise[:, :positions] - noise[:, positions:]
        )
        bar_now = alpha_bar(time_now)
        bar_next = alpha_bar(time_next)
        clean = (latent - jnp.sqrt(1.0 - bar_now) * guided) / jnp.sqrt(bar_now)
        updated = jnp.sqrt(bar_next) * clean + jnp.sqrt(1.0 - bar_next) * guided
        latent = broadcast(updated, "sect", last_index)
    channels_here = latent.shape[0] // sect_count
    own_latent = lax.dynamic_slice_in_dim(latent, section * channels_here, channels_here, 0)
    return (segment, own_latent)


def solution(mesh):
    return jax.shard_map(
        on_device,
        mesh=mesh,
        in_specs=(
            P(("sect", "batch"), None),
            P(None, "batch"),
            P(),
            P("batch"),
            P("batch", None),
            P("sect", None),
            P("sect", None),
            P(("sect", "batch"), None),
            P(),
            P(),
        ),
        out_specs=(P(("sect", "batch"), None), P("sect", "batch")),
        check_vma=False,
    )
```

profile of v0, /device:TPU:0, one launch (start us, length us, event | category | flops | bytes accessed | tf_op | source)
XLA Modules:
  0.0 147.3 jit_solution(3572738905589902597)
XLA Ops:
  7.9 3.2 %collective-permute-start = (bf16[256,640]{1,0:T(8,128)(2,1)}, bf16[256,640]{1,0:T(8,128)(2,1)}, u32[]{:S(2)}, u32[]{:S(2)}) collective-permute-start(bf16[256,640]{1,0:T(8,128)(2,1)} %param.10), channel_id=1, source_target_pairs={{0,8},{8,16},{16,24},{1,9},{9,17},{17,25},{2,10},{10,18},{18,26},{... | collective-permute-start | bytes 983048 | tf_op jit(solution)/shard_map/ppermute | solution.py:13
  11.8 1.5 %fusion.362 = (s32[1]{0:T(128)}, s32[1]{0:T(128)}, s32[1]{0:T(128)}, s32[1]{0:T(128)}, s32[1]{0:T(128)}) fusion(s32[5]{0:T(128)} %param.12), kind=kLoop, calls=%fused_computation.457 | loop fusion | bytes 40 | tf_op jit(solution)/shard_map/slice | solution.py:83
  18.7 31.3 %all-gather = bf16[8,1,640]{2,1,0:T(2,128)(2,1)S(1)} all-gather(bf16[1,1,640]{2,1,0:T(2,128)(2,1)} %bitcast.47), channel_id=1, replica_groups=mesh['sect'=4,'batch'=8] {'batch'}, dimensions={0}, use_global_device_ids=true | all-gather | bytes 11520 | tf_op jit(solution)/shard_map/all_gather | solution.py:63
  50.0 1.4 convolution_reduce_fusion.4
  51.4 1.4 convolution_reduce_fusion.3
  53.8 1.4 multiply_reduce_fusion.3
  55.2 3.8 %fusion.196 = f32[256,2560]{1,0:T(8,128)} fusion(bf16[640,2560]{1,0:T(8,128)(2,1)S(1)} %copy-done, f32[256]{0:T(256)S(1)} %add_rsqrt_fusion.7, f32[128,640]{1,0:T(8,128)S(1)} %broadcast_in_dim.2, bf16[256,640]{1,0:T(8,128)(2,1)} %collective-permute-done.1, bf16[256,640]{1,0:T(8,128)(2,1)} %collective-permute-done, ...), kind=kOutput, calls=%fused_computation.265 | convolution fusion | flops 840990720 | bytes 7048705 | tf_op jit(solution)/shard_map/dot_general | solution.py:46
  59.0 6.4 %fusion.72 = (f32[256]{0:T(256)S(1)}, bf16[256,640]{1,0:T(8,128)(2,1)}) fusion(bf16[1280,640]{1,0:T(8,128)(2,1)} %all-gather.3.cloned.1.call-done, f32[256,2560]{1,0:T(8,128)} %fusion.196, f32[128,640]{1,0:T(8,128)} %copy-done.1, f32[640]{0:T(1024)S(1)} %convolution_reduce_fusion.4, bf16[256,640]{1,0:T(8,128)(2,1)} %collective-permute-done.1, ...), kind=kOutput, calls=%fused_computation.137 | convolution fusion | flops 443678464 | bytes 5737985 | tf_op jit(solution)/shard_map/dot_general | solution.py:50
  65.4 2.0 %collective-permute-start.2 = (bf16[256,640]{1,0:T(8,128)(2,1)}, bf16[256,640]{1,0:T(8,128)(2,1)}, u32[]{:S(2)}, u32[]{:S(2)}) collective-permute-start(bf16[256,640]{1,0:T(8,128)(2,1)} %get-tuple-element.8), channel_id=1, source_target_pairs={{0,8},{8,16},{16,24},{1,9},{9,17},{17,25},{2,10},{10,18},{18,26},{... | collective-permute-start | bytes 983048 | tf_op jit(solution)/shard_map/ppermute | solution.py:13
  68.8 9.1 %psum.28 = f32[4,128]{1,0:T(4,128)S(1)} all-reduce(f32[4,128]{1,0:T(4,128)S(1)} %add_select_fusion.3), channel_id=1, replica_groups=mesh['sect'=4,'batch'=8] {'sect'}, use_global_device_ids=true, to_apply=%region_2.3 | all-reduce | flops 512 | bytes 4096 | tf_op jit(solution)/shard_map/psum | solution.py:24
  78.2 1.4 multiply_reduce_fusion.2
  79.6 2.4 %fusion.197 = f32[256,2560]{1,0:T(8,128)S(1)} fusion(bf16[640,2560]{1,0:T(8,128)(2,1)S(1)} %copy-done, f32[256]{0:T(256)S(1)} %add_rsqrt_fusion.5, f32[128,640]{1,0:T(8,128)S(1)} %copy-done.2, bf16[256,640]{1,0:T(8,128)(2,1)} %collective-permute-done.3, bf16[256,640]{1,0:T(8,128)(2,1)} %collective-permute-done.2, ...), kind=kOutput, calls=%fused_computation.266 | convolution fusion | flops 840990720 | bytes 7048705 | tf_op jit(solution)/shard_map/dot_general | solution.py:46
  82.0 5.2 %fusion.73 = (f32[256]{0:T(256)S(1)}, bf16[256,640]{1,0:T(8,128)(2,1)}) fusion(bf16[1280,640]{1,0:T(8,128)(2,1)S(1)} %copy-done.8, f32[256,2560]{1,0:T(8,128)S(1)} %fusion.197, f32[128,640]{1,0:T(8,128)S(1)} %copy-done.2, f32[640]{0:T(1024)S(1)} %convolution_reduce_fusion.3, bf16[256,640]{1,0:T(8,128)(2,1)} %collective-permute-done.3, ...), kind=kOutput, calls=%fused_computation.138 | convolution fusion | flops 443678464 | bytes 5737985 | tf_op jit(solution)/shard_map/dot_general | solution.py:50
  87.2 3.0 %collective-permute-start.4 = (bf16[256,640]{1,0:T(8,128)(2,1)}, bf16[256,640]{1,0:T(8,128)(2,1)}, u32[]{:S(2)}, u32[]{:S(2)}) collective-permute-start(bf16[256,640]{1,0:T(8,128)(2,1)} %get-tuple-element.10), channel_id=1, source_target_pairs={{0,8},{8,16},{16,24},{1,9},{9,17},{17,25},{2,10},{10,18},{18,26},{... | collective-permute-start | bytes 983048 | tf_op jit(solution)/shard_map/ppermute | solution.py:13
  91.6 9.8 %psum.29 = f32[4,128]{1,0:T(4,128)S(1)} all-reduce(f32[4,128]{1,0:T(4,128)S(1)} %add_select_fusion.2), channel_id=1, replica_groups=mesh['sect'=4,'batch'=8] {'sect'}, use_global_device_ids=true, to_apply=%region_5.6 | all-reduce | flops 512 | bytes 4096 | tf_op jit(solution)/shard_map/psum | solution.py:24
  101.6 1.4 multiply_reduce_fusion.1
  103.0 2.4 %fusion.198 = f32[256,2560]{1,0:T(8,128)S(1)} fusion(bf16[640,2560]{1,0:T(8,128)(2,1)S(1)} %copy-done, f32[256]{0:T(256)S(1)} %add_rsqrt_fusion.3, f32[128,640]{1,0:T(8,128)S(1)} %copy-done.3, bf16[256,640]{1,0:T(8,128)(2,1)} %collective-permute-done.5, bf16[256,640]{1,0:T(8,128)(2,1)} %collective-permute-done.4, ...), kind=kOutput, calls=%fused_computation.267 | convolution fusion | flops 840990720 | bytes 7048705 | tf_op jit(solution)/shard_map/dot_general | solution.py:46
  105.4 5.2 %fusion.74 = (f32[256]{0:T(256)S(1)}, bf16[256,640]{1,0:T(8,128)(2,1)}) fusion(bf16[1280,640]{1,0:T(8,128)(2,1)S(1)} %copy-done.9, f32[256,2560]{1,0:T(8,128)S(1)} %fusion.198, f32[128,640]{1,0:T(8,128)S(1)} %copy-done.3, f32[640]{0:T(1024)S(1)} %convolution_reduce_fusion.2, bf16[256,640]{1,0:T(8,128)(2,1)} %collective-permute-done.5, ...), kind=kOutput, calls=%fused_computation.139 | convolution fusion | flops 443678464 | bytes 5737985 | tf_op jit(solution)/shard_map/dot_general | solution.py:50
  110.6 2.0 %collective-permute-start.6 = (bf16[256,640]{1,0:T(8,128)(2,1)}, bf16[256,640]{1,0:T(8,128)(2,1)}, u32[]{:S(2)}, u32[]{:S(2)}) collective-permute-start(bf16[256,640]{1,0:T(8,128)(2,1)} %get-tuple-element.12), channel_id=1, source_target_pairs={{0,8},{8,16},{16,24},{1,9},{9,17},{17,25},{2,10},{10,18},{18,26},{... | collective-permute-start | bytes 983048 | tf_op jit(solution)/shard_map/ppermute | solution.py:13
  114.2 10.5 %psum.30 = f32[4,128]{1,0:T(4,128)S(1)} all-reduce(f32[4,128]{1,0:T(4,128)S(1)} %add_select_fusion.1), channel_id=1, replica_groups=mesh['sect'=4,'batch'=8] {'sect'}, use_global_device_ids=true, to_apply=%region_8.9 | all-reduce | flops 512 | bytes 4096 | tf_op jit(solution)/shard_map/psum | solution.py:24
  125.0 1.4 multiply_reduce_fusion
  126.4 2.4 %fusion.199 = f32[256,2560]{1,0:T(8,128)S(1)} fusion(bf16[640,2560]{1,0:T(8,128)(2,1)S(1)} %copy-done, f32[256]{0:T(256)S(1)} %add_rsqrt_fusion.1, f32[128,640]{1,0:T(8,128)S(1)} %copy-done.4, bf16[256,640]{1,0:T(8,128)(2,1)} %collective-permute-done.7, bf16[256,640]{1,0:T(8,128)(2,1)} %collective-permute-done.6, ...), kind=kOutput, calls=%fused_computation.268 | convolution fusion | flops 840990720 | bytes 7048705 | tf_op jit(solution)/shard_map/dot_general | solution.py:46
  128.8 4.6 %fusion.75 = (f32[256]{0:T(256)S(1)}, bf16[256,640]{1,0:T(8,128)(2,1)S(1)}) fusion(bf16[1280,640]{1,0:T(8,128)(2,1)S(1)} %copy-done.10, f32[256,2560]{1,0:T(8,128)S(1)} %fusion.199, f32[128,640]{1,0:T(8,128)S(1)} %copy-done.4, f32[640]{0:T(1024)S(1)} %convolution_reduce_fusion.1, bf16[256,640]{1,0:T(8,128)(2,1)} %collective-permute-done.7, ...), kind=kOutput, calls=%fused_computation.140 | convolution fusion | flops 443678464 | bytes 5737985 | tf_op jit(solution)/shard_map/dot_general | solution.py:50
  134.2 5.8 %psum.31 = f32[4,128]{1,0:T(4,128)S(1)} all-reduce(f32[4,128]{1,0:T(4,128)S(1)} %add_select_fusion), channel_id=1, replica_groups=mesh['sect'=4,'batch'=8] {'sect'}, use_global_device_ids=true, to_apply=%region_11.12 | all-reduce | flops 512 | bytes 4096 | tf_op jit(solution)/shard_map/psum | solution.py:24
  (78 shorter events, 9.3 us)
Async XLA Ops:
  7.2 48.0 %copy-start = (bf16[640,2560]{1,0:T(8,128)(2,1)S(1)}, bf16[640,2560]{1,0:T(8,128)(2,1)}, u32[]{:S(2)}) copy-start(bf16[640,2560]{1,0:T(8,128)(2,1)} %param.15) | copy-start | bytes 9830404
  7.2 51.8 %all-gather.3.cloned.1.call-start = ((), (), s32[]{:S(2)}) async-start(), calls=%async_computation | async-start | bytes 1843200 | tf_op jit(solution)/shard_map/all_gather | solution.py:62
  7.9 45.8 %collective-permute-start = (bf16[256,640]{1,0:T(8,128)(2,1)}, bf16[256,640]{1,0:T(8,128)(2,1)}, u32[]{:S(2)}, u32[]{:S(2)}) collective-permute-start(bf16[256,640]{1,0:T(8,128)(2,1)} %param.10), channel_id=1, source_target_pairs={{0,8},{8,16},{16,24},{1,9},{9,17},{17,25},{2,10},{10,18},{18,26},{... | collective-permute-start | bytes 983048 | tf_op jit(solution)/shard_map/ppermute | solution.py:13
  11.1 42.6 %collective-permute-start.1 = (bf16[256,640]{1,0:T(8,128)(2,1)}, bf16[256,640]{1,0:T(8,128)(2,1)}, u32[]{:S(2)}, u32[]{:S(2)}) collective-permute-start(bf16[256,640]{1,0:T(8,128)(2,1)} %param.10), channel_id=1, source_target_pairs={{8,0},{16,8},{24,16},{0,24},{9,1},{17,9},{25,17},{1,25},{10,2},{18... | collective-permute-start | bytes 983048 | tf_op jit(solution)/shard_map/ppermute | solution.py:19
  18.7 34.1 %copy-start.5 = (bf16[640,640]{1,0:T(8,128)(2,1)S(1)}, bf16[640,640]{1,0:T(8,128)(2,1)}, u32[]{:S(2)}) copy-start(bf16[640,640]{1,0:T(8,128)(2,1)} %param.16) | copy-start | bytes 2457604
  51.4 2.1 %copy-start.6 = (bf16[4,640]{1,0:T(4,128)(2,1)S(1)}, bf16[4,640]{1,0:T(4,128)(2,1)}, u32[]{:S(2)}) copy-start(bf16[4,640]{1,0:T(4,128)(2,1)} %param.18) | copy-start | bytes 15364
  51.4 2.1 %copy-start.7 = (f32[4,128]{1,0:T(4,128)S(1)}, f32[4,128]{1,0:T(4,128)}, u32[]{:S(2)}) copy-start(f32[4,128]{1,0:T(4,128)} %param.11) | copy-start | bytes 6148
  53.8 1.4 copy-start.1
  59.0 8.4 %copy-start.11 = (bf16[4,640]{1,0:T(4,128)(2,1)S(1)}, bf16[4,640]{1,0:T(4,128)(2,1)}, u32[]{:S(2)}) copy-start(bf16[4,640]{1,0:T(4,128)(2,1)} %param.19) | copy-start | bytes 15364
  65.4 12.8 %collective-permute-start.2 = (bf16[256,640]{1,0:T(8,128)(2,1)}, bf16[256,640]{1,0:T(8,128)(2,1)}, u32[]{:S(2)}, u32[]{:S(2)}) collective-permute-start(bf16[256,640]{1,0:T(8,128)(2,1)} %get-tuple-element.8), channel_id=1, source_target_pairs={{0,8},{8,16},{16,24},{1,9},{9,17},{17,25},{2,10},{10,18},{18,26},{... | collective-permute-start | bytes 983048 | tf_op jit(solution)/shard_map/ppermute | solution.py:13
  67.4 10.8 %collective-permute-start.3 = (bf16[256,640]{1,0:T(8,128)(2,1)}, bf16[256,640]{1,0:T(8,128)(2,1)}, u32[]{:S(2)}, u32[]{:S(2)}) collective-permute-start(bf16[256,640]{1,0:T(8,128)(2,1)} %get-tuple-element.8), channel_id=1, source_target_pairs={{8,0},{16,8},{24,16},{0,24},{9,1},{17,9},{25,17},{1,25},{10,2},{18... | collective-permute-start | bytes 983048 | tf_op jit(solution)/shard_map/ppermute | solution.py:19
  78.0 1.6 %copy-start.2 = (f32[128,640]{1,0:T(8,128)S(1)}, f32[128,640]{1,0:T(8,128)}, u32[]{:S(2)}) copy-start(f32[128,640]{1,0:T(8,128)} %copy-done.1) | copy-start | bytes 983044
  79.6 2.4 %copy-start.8 = (bf16[1280,640]{1,0:T(8,128)(2,1)S(1)}, bf16[1280,640]{1,0:T(8,128)(2,1)}, u32[]{:S(2)}) copy-start(bf16[1280,640]{1,0:T(8,128)(2,1)} %all-gather.3.cloned.1.call-done) | copy-start | bytes 4915204
  87.2 14.4 %collective-permute-start.4 = (bf16[256,640]{1,0:T(8,128)(2,1)}, bf16[256,640]{1,0:T(8,128)(2,1)}, u32[]{:S(2)}, u32[]{:S(2)}) collective-permute-start(bf16[256,640]{1,0:T(8,128)(2,1)} %get-tuple-element.10), channel_id=1, source_target_pairs={{0,8},{8,16},{16,24},{1,9},{9,17},{17,25},{2,10},{10,18},{18,26},{... | collective-permute-start | bytes 983048 | tf_op jit(solution)/shard_map/ppermute | solution.py:13
  90.2 11.5 %collective-permute-start.5 = (bf16[256,640]{1,0:T(8,128)(2,1)}, bf16[256,640]{1,0:T(8,128)(2,1)}, u32[]{:S(2)}, u32[]{:S(2)}) collective-permute-start(bf16[256,640]{1,0:T(8,128)(2,1)} %get-tuple-element.10), channel_id=1, source_target_pairs={{8,0},{16,8},{24,16},{0,24},{9,1},{17,9},{25,17},{1,25},{10,2},{18... | collective-permute-start | bytes 983048 | tf_op jit(solution)/shard_map/ppermute | solution.py:19
  101.4 1.6 %copy-start.3 = (f32[128,640]{1,0:T(8,128)S(1)}, f32[128,640]{1,0:T(8,128)}, u32[]{:S(2)}) copy-start(f32[128,640]{1,0:T(8,128)} %copy-done.1) | copy-start | bytes 983044
  103.0 2.4 %copy-start.9 = (bf16[1280,640]{1,0:T(8,128)(2,1)S(1)}, bf16[1280,640]{1,0:T(8,128)(2,1)}, u32[]{:S(2)}) copy-start(bf16[1280,640]{1,0:T(8,128)(2,1)} %all-gather.3.cloned.1.call-done) | copy-start | bytes 4915204
  110.6 14.4 %collective-permute-start.6 = (bf16[256,640]{1,0:T(8,128)(2,1)}, bf16[256,640]{1,0:T(8,128)(2,1)}, u32[]{:S(2)}, u32[]{:S(2)}) collective-permute-start(bf16[256,640]{1,0:T(8,128)(2,1)} %get-tuple-element.12), channel_id=1, source_target_pairs={{0,8},{8,16},{16,24},{1,9},{9,17},{17,25},{2,10},{10,18},{18,26},{... | collective-permute-start | bytes 983048 | tf_op jit(solution)/shard_map/ppermute | solution.py:13
  112.6 12.4 %collective-permute-start.7 = (bf16[256,640]{1,0:T(8,128)(2,1)}, bf16[256,640]{1,0:T(8,128)(2,1)}, u32[]{:S(2)}, u32[]{:S(2)}) collective-permute-start(bf16[256,640]{1,0:T(8,128)(2,1)} %get-tuple-element.12), channel_id=1, source_target_pairs={{8,0},{16,8},{24,16},{0,24},{9,1},{17,9},{25,17},{1,25},{10,2},{18... | collective-permute-start | bytes 983048 | tf_op jit(solution)/shard_map/ppermute | solution.py:19
  124.7 1.6 %copy-start.4 = (f32[128,640]{1,0:T(8,128)S(1)}, f32[128,640]{1,0:T(8,128)}, u32[]{:S(2)}) copy-start(f32[128,640]{1,0:T(8,128)} %copy-done.1) | copy-start | bytes 983044
  126.4 2.4 %copy-start.10 = (bf16[1280,640]{1,0:T(8,128)(2,1)S(1)}, bf16[1280,640]{1,0:T(8,128)(2,1)}, u32[]{:S(2)}) copy-start(bf16[1280,640]{1,0:T(8,128)(2,1)} %all-gather.3.cloned.1.call-done) | copy-start | bytes 4915204
  133.4 0.7 copy-start.12
Sparse Core Ops, SparseCore 0:
  10.2 47.5 all-gather.2
where the time goes:
time: 148 us; the launch traced here: 147 us
  blocking collectives  66.5 us (45%)
  matrix products  41 us (28%)
  between operations  19.2 us (13%)
  starting transfers between devices  11.1 us (8%)
  other arithmetic  6.24 us (4%)
  local copies, waits for them, and re-layouts  2.51 us (2%)
    psum x4, blocking collectives, broadcast(): return lax.psum(block, axis)  35.2 us
    all_gather x1, blocking collectives, on_device(): lax.all_gather(prompts, 'batch', axis=0, tiled=True)  31.3 us
    dot_general x4, matrix products, feed_block(): jnp.dot(hidden, weight_out, preferred_element_type=jnp.float32)  21.4 us
    dot_general x4, matrix products, feed_block(): projected = jnp.dot(normed, weight_in, preferred_element_type=jnp.float32)  11 us
    ppermute x4, starting transfers between devices, passed_along(): return lax.ppermute(shard, axis, pairs)  10.2 us
    reduce_sum x4, other arithmetic, rms_norm(): jnp.mean(values * values, axis=-1, keepdims=True) + 1e-06  5.44 us
    dot_general x4, matrix products, on_device(): lax.dot_general(conv_out_w, activated, (((1,), (1,)), ((), ())), preferre...  4.33 us
    dot_general x4, matrix products, on_device(): jnp.dot(embedded[None, :], time_w, preferred_element_type=jnp.float32)  3.26 us
  transfers between devices with their start and end apart: 9, of which 0 were waited for; matrix products, arithmetic and copies ran while one was open for 11% of the time, Pallas kernels for 0%

commit v1 on v0

--- a/solution.py
+++ b/solution.py
@@ -21,7 +21,7 @@
 
 def broadcast(block, axis, source):
     block = jnp.where(lax.axis_index(axis) == source, block, jnp.zeros_like(block))
-    return lax.psum(block, axis)
+    return jnp.sum(lax.all_gather(block, axis), axis=0)
 
 
 def sinusoid(time_value, channels):

time: 148 us -> 145 us (0.980)
  blocking collectives: 66.5 us -> 61.2 us
  starting transfers between devices: 11.1 us -> 13.7 us
    psum x4 -> x0, blocking collectives: 35.2 us -> none  [broadcast(): return lax.psum(block, axis)]
    all_gather x0 -> x4, blocking collectives: none -> 29.9 us  [broadcast(): return jnp.sum(lax.all_gather(block, axis), axis=0)]
where the time goes in v1:
time: 145 us
  blocking collectives  61.2 us (42%)
  matrix products  41.1 us (28%)
  between operations  19.2 us (13%)
  starting transfers between devices  13.7 us (9%)
  other arithmetic  6.29 us (4%)
  local copies, waits for them, and re-layouts  2.51 us (2%)
    all_gather x1, blocking collectives, on_device(): lax.all_gather(prompts, 'batch', axis=0, tiled=True)  31.3 us
    all_gather x4, blocking collectives, broadcast(): return jnp.sum(lax.all_gather(block, axis), axis=0)  29.9 us
    dot_general x4, matrix products, feed_block(): jnp.dot(hidden, weight_out, preferred_element_type=jnp.float32)  21.4 us
    ppermute x4, starting transfers between devices, passed_along(): return lax.ppermute(shard, axis, pairs)  11.6 us
    dot_general x4, matrix products, feed_block(): projected = jnp.dot(normed, weight_in, preferred_element_type=jnp.float32)  11 us
    reduce_sum x4, other arithmetic, rms_norm(): jnp.mean(values * values, axis=-1, keepdims=True) + 1e-06  5.43 us
    dot_general x4, matrix products, on_device(): lax.dot_general(conv_out_w, activated, (((1,), (1,)), ((), ())), preferre...  4.33 us
    dot_general x4, matrix products, on_device(): jnp.dot(embedded[None, :], time_w, preferred_element_type=jnp.float32)  3.26 us
  transfers between devices with their start and end apart: 9, of which 0 were waited for; matrix products, arithmetic and copies ran while one was open for 11% of the time, Pallas kernels for 0%

profile of v1, /device:TPU:0, one launch (start us, length us, event | category | flops | bytes accessed | tf_op | source)
XLA Modules:
  0.0 144.7 jit_solution(18309617896258268942)
XLA Ops:
  7.9 3.2 %collective-permute-start = (bf16[256,640]{1,0:T(8,128)(2,1)}, bf16[256,640]{1,0:T(8,128)(2,1)}, u32[]{:S(2)}, u32[]{:S(2)}) collective-permute-start(bf16[256,640]{1,0:T(8,128)(2,1)} %param.10), channel_id=1, source_target_pairs={{0,8},{8,16},{16,24},{1,9},{9,17},{17,25},{2,10},{10,18},{18,26},{... | collective-permute-start | bytes 983048 | tf_op jit(solution)/shard_map/ppermute | solution.py:13
  11.8 1.5 %fusion.362 = (s32[1]{0:T(128)}, s32[1]{0:T(128)}, s32[1]{0:T(128)}, s32[1]{0:T(128)}, s32[1]{0:T(128)}) fusion(s32[5]{0:T(128)} %param.12), kind=kLoop, calls=%fused_computation.457 | loop fusion | bytes 40 | tf_op jit(solution)/shard_map/slice | solution.py:83
  18.7 31.3 %all-gather.4 = bf16[8,1,640]{2,1,0:T(2,128)(2,1)S(1)} all-gather(bf16[1,1,640]{2,1,0:T(2,128)(2,1)} %bitcast.55), channel_id=1, replica_groups=mesh['sect'=4,'batch'=8] {'batch'}, dimensions={0}, use_global_device_ids=true | all-gather | bytes 11520 | tf_op jit(solution)/shard_map/all_gather | solution.py:63
  50.0 1.4 convolution_reduce_fusion.4
  51.4 1.4 convolution_reduce_fusion.3
  53.8 1.4 multiply_reduce_fusion.3
  55.2 3.8 %fusion.196 = f32[256,2560]{1,0:T(8,128)} fusion(bf16[640,2560]{1,0:T(8,128)(2,1)S(1)} %copy-done, f32[256]{0:T(256)S(1)} %add_rsqrt_fusion.7, f32[128,640]{1,0:T(8,128)S(1)} %broadcast_in_dim.2, bf16[256,640]{1,0:T(8,128)(2,1)} %collective-permute-done.1, bf16[256,640]{1,0:T(8,128)(2,1)} %collective-permute-done, ...), kind=kOutput, calls=%fused_computation.265 | convolution fusion | flops 840990720 | bytes 7048705 | tf_op jit(solution)/shard_map/dot_general | solution.py:46
  59.0 6.4 %fusion.72 = (f32[256]{0:T(256)S(1)}, bf16[256,640]{1,0:T(8,128)(2,1)}) fusion(bf16[1280,640]{1,0:T(8,128)(2,1)} %all-gather.11.cloned.1.call-done, f32[256,2560]{1,0:T(8,128)} %fusion.196, f32[128,640]{1,0:T(8,128)} %copy-done.1, f32[640]{0:T(1024)S(1)} %convolution_reduce_fusion.4, bf16[256,640]{1,0:T(8,128)(2,1)} %collective-permute-done.1, ...), kind=kOutput, calls=%fused_computation.137 | convolution fusion | flops 443678464 | bytes 5737985 | tf_op jit(solution)/shard_map/dot_general | solution.py:50
  65.4 2.0 %collective-permute-start.2 = (bf16[256,640]{1,0:T(8,128)(2,1)}, bf16[256,640]{1,0:T(8,128)(2,1)}, u32[]{:S(2)}, u32[]{:S(2)}) collective-permute-start(bf16[256,640]{1,0:T(8,128)(2,1)} %get-tuple-element.8), channel_id=1, source_target_pairs={{0,8},{8,16},{16,24},{1,9},{9,17},{17,25},{2,10},{10,18},{18,26},{... | collective-permute-start | bytes 983048 | tf_op jit(solution)/shard_map/ppermute | solution.py:13
  68.8 9.4 %all-gather.5 = f32[4,4,128]{2,1,0:T(4,128)S(1)} all-gather(f32[1,4,128]{2,1,0:T(4,128)S(1)} %select_bitcast_fusion.3), channel_id=2, replica_groups=mesh['sect'=4,'batch'=8] {'sect'}, dimensions={0}, use_global_device_ids=true | all-gather | bytes 10240 | tf_op jit(solution)/shard_map/all_gather | solution.py:24
  78.5 1.4 multiply_reduce_fusion.2
  79.9 2.4 %fusion.197 = f32[256,2560]{1,0:T(8,128)S(1)} fusion(bf16[640,2560]{1,0:T(8,128)(2,1)S(1)} %copy-done, f32[256]{0:T(256)S(1)} %add_rsqrt_fusion.5, f32[128,640]{1,0:T(8,128)S(1)} %copy-done.2, bf16[256,640]{1,0:T(8,128)(2,1)} %collective-permute-done.3, bf16[256,640]{1,0:T(8,128)(2,1)} %collective-permute-done.2, ...), kind=kOutput, calls=%fused_computation.266 | convolution fusion | flops 840990720 | bytes 7048705 | tf_op jit(solution)/shard_map/dot_general | solution.py:46
  82.3 5.2 %fusion.73 = (f32[256]{0:T(256)S(1)}, bf16[256,640]{1,0:T(8,128)(2,1)}) fusion(bf16[1280,640]{1,0:T(8,128)(2,1)S(1)} %copy-done.8, f32[256,2560]{1,0:T(8,128)S(1)} %fusion.197, f32[128,640]{1,0:T(8,128)S(1)} %copy-done.2, f32[640]{0:T(1024)S(1)} %convolution_reduce_fusion.3, bf16[256,640]{1,0:T(8,128)(2,1)} %collective-permute-done.3, ...), kind=kOutput, calls=%fused_computation.138 | convolution fusion | flops 443678464 | bytes 5737985 | tf_op jit(solution)/shard_map/dot_general | solution.py:50
  87.5 3.2 %collective-permute-start.4 = (bf16[256,640]{1,0:T(8,128)(2,1)}, bf16[256,640]{1,0:T(8,128)(2,1)}, u32[]{:S(2)}, u32[]{:S(2)}) collective-permute-start(bf16[256,640]{1,0:T(8,128)(2,1)} %get-tuple-element.10), channel_id=1, source_target_pairs={{0,8},{8,16},{16,24},{1,9},{9,17},{17,25},{2,10},{10,18},{18,26},{... | collective-permute-start | bytes 983048 | tf_op jit(solution)/shard_map/ppermute | solution.py:13
  92.1 6.5 %all-gather.6 = f32[4,4,128]{2,1,0:T(4,128)S(1)} all-gather(f32[1,4,128]{2,1,0:T(4,128)S(1)} %select_bitcast_fusion.2), channel_id=3, replica_groups=mesh['sect'=4,'batch'=8] {'sect'}, dimensions={0}, use_global_device_ids=true | all-gather | bytes 10240 | tf_op jit(solution)/shard_map/all_gather | solution.py:24
  98.9 1.4 multiply_reduce_fusion.1
  100.3 2.4 %fusion.198 = f32[256,2560]{1,0:T(8,128)S(1)} fusion(bf16[640,2560]{1,0:T(8,128)(2,1)S(1)} %copy-done, f32[256]{0:T(256)S(1)} %add_rsqrt_fusion.3, f32[128,640]{1,0:T(8,128)S(1)} %copy-done.3, bf16[256,640]{1,0:T(8,128)(2,1)} %collective-permute-done.5, bf16[256,640]{1,0:T(8,128)(2,1)} %collective-permute-done.4, ...), kind=kOutput, calls=%fused_computation.267 | convolution fusion | flops 840990720 | bytes 7048705 | tf_op jit(solution)/shard_map/dot_general | solution.py:46
  102.7 5.2 %fusion.74 = (f32[256]{0:T(256)S(1)}, bf16[256,640]{1,0:T(8,128)(2,1)}) fusion(bf16[1280,640]{1,0:T(8,128)(2,1)S(1)} %copy-done.9, f32[256,2560]{1,0:T(8,128)S(1)} %fusion.198, f32[128,640]{1,0:T(8,128)S(1)} %copy-done.3, f32[640]{0:T(1024)S(1)} %convolution_reduce_fusion.2, bf16[256,640]{1,0:T(8,128)(2,1)} %collective-permute-done.5, ...), kind=kOutput, calls=%fused_computation.139 | convolution fusion | flops 443678464 | bytes 5737985 | tf_op jit(solution)/shard_map/dot_general | solution.py:50
  107.9 3.1 %collective-permute-start.6 = (bf16[256,640]{1,0:T(8,128)(2,1)}, bf16[256,640]{1,0:T(8,128)(2,1)}, u32[]{:S(2)}, u32[]{:S(2)}) collective-permute-start(bf16[256,640]{1,0:T(8,128)(2,1)} %get-tuple-element.12), channel_id=1, source_target_pairs={{0,8},{8,16},{16,24},{1,9},{9,17},{17,25},{2,10},{10,18},{18,26},{... | collective-permute-start | bytes 983048 | tf_op jit(solution)/shard_map/ppermute | solution.py:13
  111.0 1.5 %collective-permute-start.7 = (bf16[256,640]{1,0:T(8,128)(2,1)}, bf16[256,640]{1,0:T(8,128)(2,1)}, u32[]{:S(2)}, u32[]{:S(2)}) collective-permute-start(bf16[256,640]{1,0:T(8,128)(2,1)} %get-tuple-element.12), channel_id=1, source_target_pairs={{8,0},{16,8},{24,16},{0,24},{9,1},{17,9},{25,17},{1,25},{10,2},{18... | collective-permute-start | bytes 983048 | tf_op jit(solution)/shard_map/ppermute | solution.py:19
  113.9 7.3 %all-gather.7 = f32[4,4,128]{2,1,0:T(4,128)S(1)} all-gather(f32[1,4,128]{2,1,0:T(4,128)S(1)} %select_bitcast_fusion.1), channel_id=4, replica_groups=mesh['sect'=4,'batch'=8] {'sect'}, dimensions={0}, use_global_device_ids=true | all-gather | bytes 10240 | tf_op jit(solution)/shard_map/all_gather | solution.py:24
  122.8 2.4 %fusion.199 = f32[256,2560]{1,0:T(8,128)S(1)} fusion(bf16[640,2560]{1,0:T(8,128)(2,1)S(1)} %copy-done, f32[256]{0:T(256)S(1)} %add_rsqrt_fusion.1, f32[128,640]{1,0:T(8,128)S(1)} %copy-done.4, bf16[256,640]{1,0:T(8,128)(2,1)} %collective-permute-done.7, bf16[256,640]{1,0:T(8,128)(2,1)} %collective-permute-done.6, ...), kind=kOutput, calls=%fused_computation.268 | convolution fusion | flops 840990720 | bytes 7048705 | tf_op jit(solution)/shard_map/dot_general | solution.py:46
  125.2 4.6 %fusion.75 = (f32[256]{0:T(256)S(1)}, bf16[256,640]{1,0:T(8,128)(2,1)S(1)}) fusion(bf16[1280,640]{1,0:T(8,128)(2,1)S(1)} %copy-done.10, f32[256,2560]{1,0:T(8,128)S(1)} %fusion.199, f32[128,640]{1,0:T(8,128)S(1)} %copy-done.4, f32[640]{0:T(1024)S(1)} %convolution_reduce_fusion.1, bf16[256,640]{1,0:T(8,128)(2,1)} %collective-permute-done.7, ...), kind=kOutput, calls=%fused_computation.140 | convolution fusion | flops 443678464 | bytes 5737985 | tf_op jit(solution)/shard_map/dot_general | solution.py:50
  130.6 6.7 %all-gather.8 = f32[4,4,128]{2,1,0:T(4,128)S(1)} all-gather(f32[1,4,128]{2,1,0:T(4,128)S(1)} %select_bitcast_fusion), channel_id=5, replica_groups=mesh['sect'=4,'batch'=8] {'sect'}, dimensions={0}, use_global_device_ids=true | all-gather | bytes 10240 | tf_op jit(solution)/shard_map/all_gather | solution.py:24
  (82 shorter events, 10.5 us)
Async XLA Ops:
  7.2 48.0 %copy-start = (bf16[640,2560]{1,0:T(8,128)(2,1)S(1)}, bf16[640,2560]{1,0:T(8,128)(2,1)}, u32[]{:S(2)}) copy-start(bf16[640,2560]{1,0:T(8,128)(2,1)} %param.15) | copy-start | bytes 9830404
  7.2 51.8 %all-gather.11.cloned.1.call-start = ((), (), s32[]{:S(2)}) async-start(), calls=%async_computation | async-start | bytes 1843200 | tf_op jit(solution)/shard_map/all_gather | solution.py:62
  7.9 45.8 %collective-permute-start = (bf16[256,640]{1,0:T(8,128)(2,1)}, bf16[256,640]{1,0:T(8,128)(2,1)}, u32[]{:S(2)}, u32[]{:S(2)}) collective-permute-start(bf16[256,640]{1,0:T(8,128)(2,1)} %param.10), channel_id=1, source_target_pairs={{0,8},{8,16},{16,24},{1,9},{9,17},{17,25},{2,10},{10,18},{18,26},{... | collective-permute-start | bytes 983048 | tf_op jit(solution)/shard_map/ppermute | solution.py:13
  11.1 42.6 %collective-permute-start.1 = (bf16[256,640]{1,0:T(8,128)(2,1)}, bf16[256,640]{1,0:T(8,128)(2,1)}, u32[]{:S(2)}, u32[]{:S(2)}) collective-permute-start(bf16[256,640]{1,0:T(8,128)(2,1)} %param.10), channel_id=1, source_target_pairs={{8,0},{16,8},{24,16},{0,24},{9,1},{17,9},{25,17},{1,25},{10,2},{18... | collective-permute-start | bytes 983048 | tf_op jit(solution)/shard_map/ppermute | solution.py:19
  18.7 34.1 %copy-start.5 = (bf16[640,640]{1,0:T(8,128)(2,1)S(1)}, bf16[640,640]{1,0:T(8,128)(2,1)}, u32[]{:S(2)}) copy-start(bf16[640,640]{1,0:T(8,128)(2,1)} %param.16) | copy-start | bytes 2457604
  51.4 2.1 %copy-start.6 = (bf16[4,640]{1,0:T(4,128)(2,1)S(1)}, bf16[4,640]{1,0:T(4,128)(2,1)}, u32[]{:S(2)}) copy-start(bf16[4,640]{1,0:T(4,128)(2,1)} %param.18) | copy-start | bytes 15364
  51.4 2.1 %copy-start.7 = (f32[4,128]{1,0:T(4,128)S(1)}, f32[4,128]{1,0:T(4,128)}, u32[]{:S(2)}) copy-start(f32[4,128]{1,0:T(4,128)} %param.11) | copy-start | bytes 6148
  53.8 1.4 copy-start.1
  59.0 8.4 %copy-start.11 = (bf16[4,640]{1,0:T(4,128)(2,1)S(1)}, bf16[4,640]{1,0:T(4,128)(2,1)}, u32[]{:S(2)}) copy-start(bf16[4,640]{1,0:T(4,128)(2,1)} %param.19) | copy-start | bytes 15364
  65.4 13.1 %collective-permute-start.2 = (bf16[256,640]{1,0:T(8,128)(2,1)}, bf16[256,640]{1,0:T(8,128)(2,1)}, u32[]{:S(2)}, u32[]{:S(2)}) collective-permute-start(bf16[256,640]{1,0:T(8,128)(2,1)} %get-tuple-element.8), channel_id=1, source_target_pairs={{0,8},{8,16},{16,24},{1,9},{9,17},{17,25},{2,10},{10,18},{18,26},{... | collective-permute-start | bytes 983048 | tf_op jit(solution)/shard_map/ppermute | solution.py:13
  67.4 11.1 %collective-permute-start.3 = (bf16[256,640]{1,0:T(8,128)(2,1)}, bf16[256,640]{1,0:T(8,128)(2,1)}, u32[]{:S(2)}, u32[]{:S(2)}) collective-permute-start(bf16[256,640]{1,0:T(8,128)(2,1)} %get-tuple-element.8), channel_id=1, source_target_pairs={{8,0},{16,8},{24,16},{0,24},{9,1},{17,9},{25,17},{1,25},{10,2},{18... | collective-permute-start | bytes 983048 | tf_op jit(solution)/shard_map/ppermute | solution.py:19
  78.2 1.6 %copy-start.2 = (f32[128,640]{1,0:T(8,128)S(1)}, f32[128,640]{1,0:T(8,128)}, u32[]{:S(2)}) copy-start(f32[128,640]{1,0:T(8,128)} %copy-done.1) | copy-start | bytes 983044
  79.9 2.4 %copy-start.8 = (bf16[1280,640]{1,0:T(8,128)(2,1)S(1)}, bf16[1280,640]{1,0:T(8,128)(2,1)}, u32[]{:S(2)}) copy-start(bf16[1280,640]{1,0:T(8,128)(2,1)} %all-gather.11.cloned.1.call-done) | copy-start | bytes 4915204
  87.5 11.4 %collective-permute-start.4 = (bf16[256,640]{1,0:T(8,128)(2,1)}, bf16[256,640]{1,0:T(8,128)(2,1)}, u32[]{:S(2)}, u32[]{:S(2)}) collective-permute-start(bf16[256,640]{1,0:T(8,128)(2,1)} %get-tuple-element.10), channel_id=1, source_target_pairs={{0,8},{8,16},{16,24},{1,9},{9,17},{17,25},{2,10},{10,18},{18,26},{... | collective-permute-start | bytes 983048 | tf_op jit(solution)/shard_map/ppermute | solution.py:13
  90.7 8.2 %collective-permute-start.5 = (bf16[256,640]{1,0:T(8,128)(2,1)}, bf16[256,640]{1,0:T(8,128)(2,1)}, u32[]{:S(2)}, u32[]{:S(2)}) collective-permute-start(bf16[256,640]{1,0:T(8,128)(2,1)} %get-tuple-element.10), channel_id=1, source_target_pairs={{8,0},{16,8},{24,16},{0,24},{9,1},{17,9},{25,17},{1,25},{10,2},{18... | collective-permute-start | bytes 983048 | tf_op jit(solution)/shard_map/ppermute | solution.py:19
  98.7 1.6 %copy-start.3 = (f32[128,640]{1,0:T(8,128)S(1)}, f32[128,640]{1,0:T(8,128)}, u32[]{:S(2)}) copy-start(f32[128,640]{1,0:T(8,128)} %copy-done.1) | copy-start | bytes 983044
  100.3 2.4 %copy-start.9 = (bf16[1280,640]{1,0:T(8,128)(2,1)S(1)}, bf16[1280,640]{1,0:T(8,128)(2,1)}, u32[]{:S(2)}) copy-start(bf16[1280,640]{1,0:T(8,128)(2,1)} %all-gather.11.cloned.1.call-done) | copy-start | bytes 4915204
  107.9 13.5 %collective-permute-start.6 = (bf16[256,640]{1,0:T(8,128)(2,1)}, bf16[256,640]{1,0:T(8,128)(2,1)}, u32[]{:S(2)}, u32[]{:S(2)}) collective-permute-start(bf16[256,640]{1,0:T(8,128)(2,1)} %get-tuple-element.12), channel_id=1, source_target_pairs={{0,8},{8,16},{16,24},{1,9},{9,17},{17,25},{2,10},{10,18},{18,26},{... | collective-permute-start | bytes 983048 | tf_op jit(solution)/shard_map/ppermute | solution.py:13
  111.0 10.4 %collective-permute-start.7 = (bf16[256,640]{1,0:T(8,128)(2,1)}, bf16[256,640]{1,0:T(8,128)(2,1)}, u32[]{:S(2)}, u32[]{:S(2)}) collective-permute-start(bf16[256,640]{1,0:T(8,128)(2,1)} %get-tuple-element.12), channel_id=1, source_target_pairs={{8,0},{16,8},{24,16},{0,24},{9,1},{17,9},{25,17},{1,25},{10,2},{18... | collective-permute-start | bytes 983048 | tf_op jit(solution)/shard_map/ppermute | solution.py:19
  121.2 1.6 %copy-start.4 = (f32[128,640]{1,0:T(8,128)S(1)}, f32[128,640]{1,0:T(8,128)}, u32[]{:S(2)}) copy-start(f32[128,640]{1,0:T(8,128)} %copy-done.1) | copy-start | bytes 983044
  122.8 2.4 %copy-start.10 = (bf16[1280,640]{1,0:T(8,128)(2,1)S(1)}, bf16[1280,640]{1,0:T(8,128)(2,1)}, u32[]{:S(2)}) copy-start(bf16[1280,640]{1,0:T(8,128)(2,1)} %all-gather.11.cloned.1.call-done) | copy-start | bytes 4915204
  129.9 0.7 copy-start.12
Sparse Core Ops, SparseCore 0:
  10.2 47.5 all-gather.10
